TPU v7x, 32 devices: a whole 2x2x4 slice. The times are simulated.
32 devices in a mesh: gx: 2 (over y), gy: 4 (over z), gz: 4 (over x, core).
Axes of the slice: x: 2, y: 2, z: 4, core: 2. Of those that a mesh axis runs over, the one named last changes fastest.
Arguments:
- offsets: float32 [3, 8, 16, 16, 128], P(None, 'gx', 'gy', 'gz'), may hold values from 0 to 1
- burgers: float32 [3, 8, 16, 16, 128], P(None, 'gx', 'gy', 'gz'), may hold values from -6 to 6
- lines: float32 [3, 8, 16, 16, 128], P(None, 'gx', 'gy', 'gz'), may hold values from -3 to 3
- counts: int32 [8, 16, 16], P('gx', 'gy', 'gz'), may hold values from 1 to 128
- connect: int32 [2, 8, 16, 16, 128], P(None, 'gx', 'gy', 'gz'), may hold values from 0 to 8191
- node_pos: float32 [3, 2, 4, 4, 8192], P(None, 'gx', 'gy', 'gz'), may hold values from -6 to 6
- drag: float32 [2, 4, 4, 8192], P('gx', 'gy', 'gz'), may hold values from 0.5 to 4
- stress: float32 [3, 3], replicated, may hold values from -1 to 1
- shifts: int32 [2, 2, 4, 4], replicated, may hold values from 0 to 512, as said below
Outputs:
- migrated: float32 [6, 2, 4, 4, 9216], P(None, 'gx', 'gy', 'gz')
Inputs may be any that keep to these rules, and one draw needn't show every extreme that they name: shifts[0] of the last domain along gx is 0 and shifts[1] of the first is 0; 512 is reached by both rows in every draw.
All inputs are finite; a program needn't handle non-finite values.
Results may differ from a plain program's by a relative error of at most 0.0003.
Values sent between devices are 32-bit elements; how exact they have to be, the bound alone decides.
A program may use at most 64 MiB of HBM per device.

v0:
```python
import jax
import jax.numpy as jnp
from jax import lax
from jax.sharding import PartitionSpec as P

MIG = 512


SOFTEN_NEAR = 0.25
SOFTEN_FAR = 4.0
NEAR_SCALE = 0.0625
FAR_SCALE = 0.03125
TIME_STEP = 0.1
NEIGHBOURS = ((1, 0, 0), (-1, 0, 0), (0, 1, 0), (0, -1, 0), (0, 0, 1), (0, 0, -1))


def with_halo(cells, sides, width):
    for axis, dim in sides:
        count = lax.axis_size(axis)
        ends = count - 1
        head = lax.slice_in_dim(cells, 0, width, axis=dim)
        tail = lax.slice_in_dim(cells, cells.shape[dim] - width, cells.shape[dim], axis=dim)
        cells = jnp.concatenate(
            [
                lax.ppermute(tail, axis, [(i, (i + 1) % count) for i in range(ends)]),
                cells,
                lax.ppermute(head, axis, [((i + 1) % count, i) for i in range(ends)]),
            ],
            axis=dim,
        )
    return cells


def passed_along(array, axis, by):
    count = lax.axis_size(axis)
    pairs = [(i, i + by) for i in range(count) if 0 <= i + by < count]
    return lax.ppermute(array, axis, pairs)


def pair_term(target, source, offset):
    deltas = [
        target[axis_id][..., :, None] - source[axis_id][..., None, :] - float(offset[axis_id])
        for axis_id in range(3)
    ]
    radius = deltas[0] * deltas[0] + deltas[1] * deltas[1] + deltas[2] * deltas[2] + SOFTEN_NEAR
    inverse = lax.rsqrt(radius)
    burgers_dot = (
        target[3][..., :, None] * source[3][..., None, :]
        + target[4][..., :, None] * source[4][..., None, :]
        + target[5][..., :, None] * source[5][..., None, :]
    )
    line_dot = (
        target[6][..., :, None] * source[6][..., None, :]
        + target[7][..., :, None] * source[7][..., None, :]
        + target[8][..., :, None] * source[8][..., None, :]
    )
    weight = burgers_dot * line_dot * inverse * inverse * inverse
    return jnp.stack([jnp.sum(weight * deltas[axis_id], axis=-1) for axis_id in range(3)])


def far_stress(moments, centers, cells):
    distance = SOFTEN_FAR + jnp.zeros((cells.shape[1], centers.shape[1]), jnp.float32)
    for axis_id in range(3):
        gap = cells[axis_id][:, None] - centers[axis_id][None, :]
        distance = distance + gap * gap
    weights = lax.rsqrt(distance)
    return jnp.dot(
        moments, weights.T, precision=lax.Precision.HIGHEST, preferred_element_type=jnp.float32
    )


def segment_force(target, sigma):
    burgers = target[3:6]
    line = target[6:9]
    pulled = [
        sigma[row, 0][..., None] * burgers[0]
        + sigma[row, 1][..., None] * burgers[1]
        + sigma[row, 2][..., None] * burgers[2]
        for row in range(3)
    ]
    return jnp.stack(
        [
            pulled[1] * line[2] - pulled[2] * line[1],
            pulled[2] * line[0] - pulled[0] * line[2],
            pulled[0] * line[1] - pulled[1] * line[0],
        ]
    )


def coarse_moments(stacked):
    product = jnp.einsum(
        "axyzk,bxyzk->abxyz", stacked[3:6], stacked[6:9], precision=lax.Precision.HIGHEST
    )
    sx, sy, sz = (product.shape[2], product.shape[3], product.shape[4])
    return product.reshape(9, sx // 2, 2, sy // 2, 2, sz // 2, 2).sum(axis=(2, 4, 6))


def window(padded, starts, grid):
    return lax.slice(
        padded,
        (0, starts[0], starts[1], starts[2], 0),
        (
            padded.shape[0],
            starts[0] + grid[0],
            starts[1] + grid[1],
            starts[2] + grid[2],
            padded.shape[4],
        ),
    )


def shards(offsets, burgers, lines, counts, connect, node_pos, drag, stress, shifts):
    size_x, size_y, size_z, slots = (
        offsets.shape[1],
        offsets.shape[2],
        offsets.shape[3],
        offsets.shape[4],
    )
    grid = (size_x, size_y, size_z)
    index_x = lax.axis_index("gx")
    index_y = lax.axis_index("gy")
    index_z = lax.axis_index("gz")
    count_x = lax.axis_size("gx")
    count_y = lax.axis_size("gy")
    count_z = lax.axis_size("gz")
    mask = (lax.broadcasted_iota(jnp.int32, grid + (slots,), 3) < counts[..., None]).astype(
        jnp.float32
    )
    stacked = jnp.concatenate([offsets, burgers * mask[None], lines], axis=0)
    near = pair_term(stacked, stacked, (0, 0, 0))
    padded = with_halo(stacked, (("gx", 1), ("gy", 2), ("gz", 3)), 1)
    for offset in NEIGHBOURS:
        source = window(padded, (1 + offset[0], 1 + offset[1], 1 + offset[2]), grid)
        near = near + pair_term(stacked, source, offset)
    own_moments = coarse_moments(stacked)
    half_x, half_y, half_z = (size_x // 2, size_y // 2, size_z // 2)
    local_count = half_x * half_y * half_z
    pieces = lax.all_gather(
        own_moments.reshape(9, 1, local_count), ("gx", "gy", "gz"), axis=1, tiled=True
    )
    devices_all = pieces.shape[1]
    moments = pieces.reshape(9, -1)
    device_ids = lax.broadcasted_iota(jnp.int32, (devices_all, local_count), 0)
    local_ids = lax.broadcasted_iota(jnp.int32, (devices_all, local_count), 1)
    slab = device_ids // (count_y * count_z)
    column = device_ids // count_z % count_y
    layer = device_ids % count_z
    coarse_x = slab * half_x + local_ids // (half_y * half_z)
    coarse_y = column * half_y + local_ids // half_z % half_y
    coarse_z = layer * half_z + local_ids % half_z
    centers = jnp.stack(
        [
            (2 * coarse_x + 1).astype(jnp.float32).reshape(-1),
            (2 * coarse_y + 1).astype(jnp.float32).reshape(-1),
            (2 * coarse_z + 1).astype(jnp.float32).reshape(-1),
        ]
    )
    starts = (index_x * size_x, index_y * size_y, index_z * size_z)
    cells = jnp.stack(
        [
            (lax.broadcasted_iota(jnp.int32, grid, axis_id) + starts[axis_id])
            .astype(jnp.float32)
            .reshape(-1)
            + 0.5
            for axis_id in range(3)
        ]
    )
    sigma = (
        FAR_SCALE * far_stress(moments, centers, cells).reshape(3, 3, size_x, size_y, size_z)
        + stress[:, :, None, None, None]
    )
    total = NEAR_SCALE * near + segment_force(stacked, sigma)
    nodes = node_pos.shape[4]
    margin = MIG
    halves = 0.5 * total.reshape(3, -1)
    values = jnp.concatenate([halves, halves], axis=1).T
    node_force = jax.ops.segment_sum(values, connect.reshape(-1), num_segments=nodes).T
    velocity = node_force / drag.reshape(1, nodes)
    fields = jnp.concatenate([node_pos.reshape(3, nodes) + TIME_STEP * velocity, velocity], axis=0)
    from_below = passed_along(fields[:, nodes - margin :], "gx", 1)
    from_above = passed_along(fields[:, :margin], "gx", -1)
    sectioning = jnp.concatenate([from_below, fields, from_above], axis=1)
    capacity = sectioning.shape[1]
    up_own = shifts[0][index_x, index_y, index_z]
    down_own = shifts[1][index_x, index_y, index_z]
    up_prev = jnp.where(index_x > 0, shifts[0][jnp.maximum(index_x - 1, 0), index_y, index_z], 0)
    down_next = jnp.where(
        index_x < count_x - 1, shifts[1][jnp.minimum(index_x + 1, count_x - 1), index_y, index_z], 0
    )
    position = lax.broadcasted_iota(jnp.int32, (capacity,), 0)
    kept = nodes - up_own - down_own
    source = jnp.where(
        position < up_prev,
        margin - up_prev + position,
        jnp.where(
            position < up_prev + kept,
            margin + down_own + position - up_prev,
            margin + nodes + position - up_prev - kept,
        ),
    )
    source = jnp.clip(source, 0, capacity - 1)
    live = position < up_prev + kept + down_next
    result = jnp.where(live[None], jnp.take(sectioning, source, axis=1), 0.0)
    return result.reshape(6, 1, 1, 1, capacity)


def solution(mesh):
    return jax.shard_map(
        shards,
        mesh=mesh,
        in_specs=(
            P(None, "gx", "gy", "gz", None),
            P(None, "gx", "gy", "gz", None),
            P(None, "gx", "gy", "gz", None),
            P("gx", "gy", "gz"),
            P(None, "gx", "gy", "gz", None),
            P(None, "gx", "gy", "gz", None),
            P("gx", "gy", "gz", None),
            P(),
            P(),
        ),
        out_specs=P(None, "gx", "gy", "gz", None),
        check_vma=False,
    )
```

profile of v0, /device:TPU:0, one launch (start us, length us, event | category | flops | bytes accessed | tf_op | source)
XLA Modules:
  0.0 343.4 jit_solution(17217576920003410518)
XLA Ops:
  0.9 0.9 copy.127
  1.8 0.9 copy.136
  2.7 0.9 copy_multiply_fusion
  3.7 1.3 collective-permute-start
  5.0 4.9 %collective-permute-start.1 = (f32[9,1,4,4,128]{4,2,3,1,0:T(4,128)S(1)}, f32[9,1,4,4,128]{4,2,3,1,0:T(4,128)S(1)}, u32[]{:S(2)}, u32[]{:S(2)}) collective-permute-start(f32[9,1,4,4,128]{4,2,3,1,0:T(4,128)S(1)} %get-tuple-element.96), channel_id=1, source_target_pairs={{0,16},{1,17},{2,18},{3,19},{4,20},{5,21},{6,22},{7,23},{8,24},{9,... | collective-permute-start | bytes 221192 | tf_op jit(solution)/shard_map/ppermute | solution.py:25
  9.9 1.5 convolution_bitcast_fusion
  11.6 0.8 slice_bitcast_fusion.19
  12.5 41.1 %all_gather.3 = f32[9,32,8]{0,2,1:T(8,128)S(1)} all-gather(f32[9,1,8]{0,2,1:T(8,128)S(1)} %bitcast.225), channel_id=1, replica_groups=mesh['gx'=2,'gy'=4,'gz'=4] {'gx','gy','gz'}, dimensions={1}, use_global_device_ids=true | all-gather | bytes 9504 | tf_op jit(solution)/shard_map/all_gather | solution.py:138
  54.8 1.8 fusion.46
  61.8 3.4 copy.118
  66.9 1.3 collective-permute-start.2
  68.2 4.6 %collective-permute-start.3 = (f32[9,6,1,4,128]{4,2,3,1,0:T(1,128)S(1)}, f32[9,6,1,4,128]{4,2,3,1,0:T(1,128)S(1)}, u32[]{:S(2)}, u32[]{:S(2)}) collective-permute-start(f32[9,6,1,4,128]{4,2,3,1,0:T(1,128)S(1)} %get-tuple-element.76), channel_id=1, source_target_pairs={{0,4},{4,8},{8,12},{1,5},{5,9},{9,13},{2,6},{6,10},{10,14},{3,7},{... | collective-permute-start | bytes 331784 | tf_op jit(solution)/shard_map/ppermute | solution.py:25
  72.9 15.1 %multiply_reduce_fusion.5 = (f32[4,4,4,128]{3,2,1,0:T(4,128)S(1)}, f32[4,4,4,128]{3,2,1,0:T(4,128)S(1)}, f32[4,4,4,128]{3,2,1,0:T(4,128)S(1)}) fusion(f32[4,4,4,128]{3,2,1,0:T(4,128)S(1)} %copy.144, f32[4,4,4,128]{3,2,1,0:T(4,128)S(1)} %get-tuple-element.110, f32[4,4,4,128]{3,2,1,0:T(4,128)S(1)} %copy.146, f32[4,4,4,128]{3,2,1,0:T(4,128)S(1)} %get-tuple-element.111, ...), kind=kLoop, calls=%fused_computation.96 | loop fusion | flops 31432704 | bytes 688128 | tf_op jit(solution)/shard_map/reduce_sum | solution.py:58
  87.9 15.1 %multiply_reduce_fusion.4 = (f32[4,4,4,128]{3,2,1,0:T(4,128)S(1)}, f32[4,4,4,128]{3,2,1,0:T(4,128)S(1)}, f32[4,4,4,128]{3,2,1,0:T(4,128)S(1)}) fusion(f32[4,4,4,128]{3,2,1,0:T(4,128)S(1)} %copy.153, f32[4,4,4,128]{3,2,1,0:T(4,128)S(1)} %get-tuple-element.110, f32[4,4,4,128]{3,2,1,0:T(4,128)S(1)} %copy.155, f32[4,4,4,128]{3,2,1,0:T(4,128)S(1)} %get-tuple-element.111, ...), kind=kLoop, calls=%fused_computation.94 | loop fusion | flops 31432704 | bytes 688128 | tf_op jit(solution)/shard_map/reduce_sum | solution.py:58
  104.0 1.3 collective-permute-start.4
  105.3 3.2 collective-permute-start.5
  108.5 15.0 %fusion.24 = (f32[4,4,4,128]{3,2,1,0:T(4,128)S(1)}, f32[4,4,4,128]{3,2,1,0:T(4,128)S(1)}, f32[4,4,4,128]{3,2,1,0:T(4,128)S(1)}) fusion(f32[4,4,4,128]{3,2,1,0:T(4,128)S(1)} %copy.162, f32[4,4,4,128]{3,2,1,0:T(4,128)S(1)} %get-tuple-element.110, f32[4,4,4,128]{3,2,1,0:T(4,128)S(1)} %copy.164, f32[4,4,4,128]{3,2,1,0:T(4,128)S(1)} %get-tuple-element.111, ...), kind=kLoop, calls=%fused_computation.64 | loop fusion | flops 31432704 | bytes 688128 | tf_op jit(solution)/shard_map/reduce_sum | solution.py:58
  123.6 15.0 %fusion.30 = (f32[4,4,4,128]{3,2,1,0:T(4,128)S(1)}, f32[4,4,4,128]{3,2,1,0:T(4,128)S(1)}, f32[4,4,4,128]{3,2,1,0:T(4,128)S(1)}) fusion(f32[4,4,4,128]{3,2,1,0:T(4,128)S(1)} %copy.171, f32[4,4,4,128]{3,2,1,0:T(4,128)S(1)} %get-tuple-element.110, f32[4,4,4,128]{3,2,1,0:T(4,128)S(1)} %copy.173, f32[4,4,4,128]{3,2,1,0:T(4,128)S(1)} %get-tuple-element.111, ...), kind=kLoop, calls=%fused_computation.70 | loop fusion | flops 31432704 | bytes 688128 | tf_op jit(solution)/shard_map/reduce_sum | solution.py:58
  139.8 15.1 %fusion.36 = (f32[4,4,4,128]{3,2,1,0:T(4,128)S(1)}, f32[4,4,4,128]{3,2,1,0:T(4,128)S(1)}, f32[4,4,4,128]{3,2,1,0:T(4,128)S(1)}) fusion(f32[4,4,4,128]{3,2,1,0:T(4,128)S(1)} %copy.180, f32[4,4,4,128]{3,2,1,0:T(4,128)S(1)} %get-tuple-element.110, f32[4,4,4,128]{3,2,1,0:T(4,128)S(1)} %copy.182, f32[4,4,4,128]{3,2,1,0:T(4,128)S(1)} %get-tuple-element.111, ...), kind=kLoop, calls=%fused_computation.76 | loop fusion | flops 31432704 | bytes 688128 | tf_op jit(solution)/shard_map/reduce_sum | solution.py:58
  154.9 18.8 %fusion.5 = (f32[4,4,4,128]{3,2,1,0:T(4,128)S(1)}, f32[4,4,4,128]{3,2,1,0:T(4,128)S(1)}, f32[4,4,4,128]{3,2,1,0:T(4,128)S(1)}, f32[4,4,4,128]{3,2,1,0:T(4,128)S(...) fusion(f32[4,4,4,128]{3,2,1,0:T(4,128)S(1)} %get-tuple-element.110, ...), kind=kLoop, calls=%fused_computation.45 | loop fusion | flops 61816832 | bytes 786432 | tf_op jit(solution)/shard_map/reduce_sum | solution.py:58
  174.5 5.1 %copy.207 = f32[16384,3]{1,0:T(8,128)} copy(f32[16384,3]{0,1:T(4,128)S(1)} %maximum_bitcast_fusion) | data formatting | bytes 393216 | tf_op jit(solution)/shard_map/transpose | solution.py:176
  179.6 89.8 %scatter_custom_fusion = f32[8192,3]{1,0:T(8,128)} fusion(s32[16384]{0:T(1024)} %bitcast.226, f32[16384,3]{1,0:T(8,128)} %copy.207, f32[]{:T(128)} %constant.148.clone.1), kind=kCustom, calls=%fused_computation.98 | custom fusion | flops 49152 | bytes 98816 | tf_op jit(solution)/shard_map/scatter-add | solution.py:177
  269.4 6.1 %bitcast_add_fusion = (f32[3,8192]{0,1:T(8,128)}, f32[3,8192]{0,1:T(8,128)}) fusion(f32[3,1,1,1,8192]{0,4,3,2,1:T(8,128)} %copy.118, f32[8192,3]{1,0:T(8,128)} %scatter_custom_fusion, f32[8192]{0:T(1024)S(1)} %bitcast.194), kind=kLoop, calls=%fused_computation.84 | loop fusion | flops 73728 | bytes 425984 | tf_op jit(solution)/shard_map/add | solution.py:179
  275.4 2.8 copy.208
  278.3 2.9 copy.209
  281.2 4.6 %collective-permute-start.6 = (f32[6,512]{1,0:T(8,128)S(1)}, f32[6,512]{1,0:T(8,128)S(1)}, u32[]{:S(2)}, u32[]{:S(2)}) collective-permute-start(f32[6,512]{1,0:T(8,128)S(1)} %get-tuple-element.98), channel_id=1, source_target_pairs={{0,16},{1,17},{2,18},{3,19},{4,20},{5,21},{6,22},{7,23},{8,24},{9,... | collective-permute-start | bytes 36872 | tf_op jit(solution)/shard_map/ppermute | solution.py:37
  285.7 1.3 collective-permute-start.7
  287.2 4.2 %collective-permute-done.7 = f32[6,512]{1,0:T(8,128)S(1)} collective-permute-done((f32[6,512]{1,0:T(8,128)S(1)}, f32[6,512]{1,0:T(8,128)S(1)}, u32[]{:S(2)}, u32[]{:S(2)}) %collective-permute-start.7) | collective-permute-done | bytes 12320 | tf_op jit(solution)/shard_map/ppermute | solution.py:37
  291.4 2.9 copy.210
  294.3 33.3 %gather_fusion = f32[9216,6]{1,0:T(8,128)} fusion(f32[6,9216]{0,1:T(8,128)} %copy.210, s32[9216]{0:T(1024)S(1)} %broadcast_clamp_fusion), kind=kCustom, calls=%fused_computation | custom fusion | bytes 479232 | tf_op jit(solution)/shard_map/jit(_take)/gather | solution.py:203
  327.6 11.3 %fusion = f32[6,1,1,1,9216]{0,4,3,2,1:T(8,128)} fusion(f32[9216,6]{1,0:T(8,128)} %gather_fusion, pred[9216]{0:T(1024)(128)(4,1)S(1)} %compare_and_fusion, pred[9216]{0:T(1024)(128)(4,1)S(1)} %iota_compare_fusion.2), kind=kLoop, calls=%fused_computation.40 | loop fusion | flops 110592 | bytes 460800 | tf_op jit(solution)/shard_map/jit(_where)/select_n | solution.py:203
  339.0 4.5 %copy.211 = f32[6,1,1,1,9216]{4,3,2,1,0:T(1,128)} copy(f32[6,1,1,1,9216]{0,4,3,2,1:T(8,128)} %fusion) | data formatting | bytes 442368 | tf_op jit(solution)/shard_map/jit(_where)/select_n | solution.py:203
  (137 shorter events, 8.3 us)
Async XLA Ops:
  3.7 62.2 %collective-permute-start = (f32[9,1,4,4,128]{4,2,3,1,0:T(4,128)S(1)}, f32[9,1,4,4,128]{4,2,3,1,0:T(4,128)S(1)}, u32[]{:S(2)}, u32[]{:S(2)}) collective-permute-start(f32[9,1,4,4,128]{4,2,3,1,0:T(4,128)S(1)} %get-tuple-element.97), channel_id=1, source_target_pairs={{16,0},{17,1},{18,2},{19,3},{20,4},{21,5},{22,6},{23,7},{24,8},{25... | collective-permute-start | bytes 221192 | tf_op jit(solution)/shard_map/ppermute | solution.py:27
  5.0 60.9 %collective-permute-start.1 = (f32[9,1,4,4,128]{4,2,3,1,0:T(4,128)S(1)}, f32[9,1,4,4,128]{4,2,3,1,0:T(4,128)S(1)}, u32[]{:S(2)}, u32[]{:S(2)}) collective-permute-start(f32[9,1,4,4,128]{4,2,3,1,0:T(4,128)S(1)} %get-tuple-element.96), channel_id=1, source_target_pairs={{0,16},{1,17},{2,18},{3,19},{4,20},{5,21},{6,22},{7,23},{8,24},{9,... | collective-permute-start | bytes 221192 | tf_op jit(solution)/shard_map/ppermute | solution.py:25
  66.9 36.3 %collective-permute-start.2 = (f32[9,6,1,4,128]{4,2,3,1,0:T(1,128)S(1)}, f32[9,6,1,4,128]{4,2,3,1,0:T(1,128)S(1)}, u32[]{:S(2)}, u32[]{:S(2)}) collective-permute-start(f32[9,6,1,4,128]{4,2,3,1,0:T(1,128)S(1)} %get-tuple-element.77), channel_id=1, source_target_pairs={{4,0},{8,4},{12,8},{5,1},{9,5},{13,9},{6,2},{10,6},{14,10},{7,3},{... | collective-permute-start | bytes 331784 | tf_op jit(solution)/shard_map/ppermute | solution.py:27
  68.2 35.3 %collective-permute-start.3 = (f32[9,6,1,4,128]{4,2,3,1,0:T(1,128)S(1)}, f32[9,6,1,4,128]{4,2,3,1,0:T(1,128)S(1)}, u32[]{:S(2)}, u32[]{:S(2)}) collective-permute-start(f32[9,6,1,4,128]{4,2,3,1,0:T(1,128)S(1)} %get-tuple-element.76), channel_id=1, source_target_pairs={{0,4},{4,8},{8,12},{1,5},{5,9},{9,13},{2,6},{6,10},{10,14},{3,7},{... | collective-permute-start | bytes 331784 | tf_op jit(solution)/shard_map/ppermute | solution.py:25
  104.0 34.6 %collective-permute-start.4 = (f32[9,6,6,1,128]{4,2,3,1,0:T(8,128)S(1)}, f32[9,6,6,1,128]{4,2,3,1,0:T(8,128)S(1)}, u32[]{:S(2)}, u32[]{:S(2)}) collective-permute-start(f32[9,6,6,1,128]{4,2,3,1,0:T(8,128)S(1)} %get-tuple-element.56), channel_id=1, source_target_pairs={{1,0},{2,1},{3,2},{5,4},{6,5},{7,6},{9,8},{10,9},{11,10},{13,12},{... | collective-permute-start | bytes 497672 | tf_op jit(solution)/shard_map/ppermute | solution.py:27
  105.3 33.3 %collective-permute-start.5 = (f32[9,6,6,1,128]{4,2,3,1,0:T(8,128)S(1)}, f32[9,6,6,1,128]{4,2,3,1,0:T(8,128)S(1)}, u32[]{:S(2)}, u32[]{:S(2)}) collective-permute-start(f32[9,6,6,1,128]{4,2,3,1,0:T(8,128)S(1)} %get-tuple-element.57), channel_id=1, source_target_pairs={{0,1},{1,2},{2,3},{4,5},{5,6},{6,7},{8,9},{9,10},{10,11},{12,13},{... | collective-permute-start | bytes 497672 | tf_op jit(solution)/shard_map/ppermute | solution.py:25
  179.6 89.8 %copy-start = (f32[1,1,1,8192]{3,2,1,0:T(1,128)S(1)}, f32[1,1,1,8192]{3,2,1,0:T(1,128)}, u32[]{:S(2)}) copy-start(f32[1,1,1,8192]{3,2,1,0:T(1,128)} %param.15) | copy-start | bytes 98308
  281.2 6.0 %collective-permute-start.6 = (f32[6,512]{1,0:T(8,128)S(1)}, f32[6,512]{1,0:T(8,128)S(1)}, u32[]{:S(2)}, u32[]{:S(2)}) collective-permute-start(f32[6,512]{1,0:T(8,128)S(1)} %get-tuple-element.98), channel_id=1, source_target_pairs={{0,16},{1,17},{2,18},{3,19},{4,20},{5,21},{6,22},{7,23},{8,24},{9,... | collective-permute-start | bytes 36872 | tf_op jit(solution)/shard_map/ppermute | solution.py:37
  285.7 5.6 %collective-permute-start.7 = (f32[6,512]{1,0:T(8,128)S(1)}, f32[6,512]{1,0:T(8,128)S(1)}, u32[]{:S(2)}, u32[]{:S(2)}) collective-permute-start(f32[6,512]{1,0:T(8,128)S(1)} %get-tuple-element.99), channel_id=1, source_target_pairs={{16,0},{17,1},{18,2},{19,3},{20,4},{21,5},{22,6},{23,7},{24,8},{25... | collective-permute-start | bytes 36872 | tf_op jit(solution)/shard_map/ppermute | solution.py:37
where the time goes:
time: 344 us; the launch traced here: 343 us
  other arithmetic  206 us (60%)
  local copies, waits for them, and re-layouts  62.4 us (18%)
  blocking collectives  41.1 us (12%)
  starting transfers between devices  22.4 us (7%)
  waiting for transfers between devices  4.33 us (1%)
  between operations  4.25 us (1%)
    reduce_sum x6, other arithmetic, pair_term(): jnp.sum(weight * deltas[axis_id], axis=-1)  94.2 us
    scatter-add x1, other arithmetic, shards(): jax.ops.segment_sum(values, connect.reshape(-1), num_segments=nodes)  89.8 us
    all_gather x1, blocking collectives, shards(): lax.all_gather(own_moments.reshape(9, 1, local_count), ('gx', 'gy', 'gz')...  41.1 us
    gather x1, local copies, waits for them, and re-layouts, shards(): result = jnp.where(live[None], jnp.take(sectioning, source, axis=1), 0.0)  33.3 us
    ppermute x3, starting transfers between devices, with_halo(): lax.ppermute(tail, axis, [(i, (i + 1) % count) for i in range(ends)])  12.7 us
    select_n x2, other arithmetic, shards(): result = jnp.where(live[None], jnp.take(sectioning, source, axis=1), 0.0)  11.5 us
  transfers between devices with their start and end apart: 8, of which 2 were waited for; matrix products, arithmetic and copies ran while one was open for 21% of the time, Pallas kernels for 0%

commit v1 on v0

v1 whole, which is shorter than its diff:
```python
import functools

import jax
import jax.numpy as jnp
import numpy as np
from jax import lax
from jax.experimental import pallas as pl
from jax.experimental.pallas import tpu as pltpu
from jax.sharding import PartitionSpec as P

MIG = 512
SOFTEN_NEAR = 0.25
SOFTEN_FAR = 4.0
NEAR_SCALE = 0.0625
FAR_SCALE = 0.03125
TIME_STEP = 0.1
AXES = ("gx", "gy", "gz")
MESH = pl.DeviceIdType.MESH
VM = pl.BlockSpec(memory_space=pltpu.VMEM)
SM = pl.BlockSpec(memory_space=pltpu.SMEM)
LANES = 128
STEP = 16


def prep_kernel(grid, off, bur, lin, counts, code, stacked, faces_x, faces_y, faces_z, mom):
    cx, cy, cz = grid
    cells = cx * cy * cz
    live = lax.broadcasted_iota(jnp.int32, (cells, LANES), 1) < counts[...]
    for c in range(3):
        stacked[c] = off[c]
        stacked[3 + c] = jnp.where(live, bur[c], 0.0)
        stacked[6 + c] = lin[c]
    for c in range(9):
        faces_x[0, c] = stacked[c, 0 : cy * cz, :]
        faces_x[1, c] = stacked[c, cells - cy * cz : cells, :]
        for x in range(cx):
            base = x * cy * cz
            faces_y[0, c, x * cz : (x + 1) * cz, :] = stacked[c, base : base + cz, :]
            base = base + (cy - 1) * cz
            faces_y[1, c, x * cz : (x + 1) * cz, :] = stacked[c, base : base + cz, :]
        faces_z[0, c] = stacked[c, pl.ds(0, cx * cy, stride=cz), :]
        faces_z[1, c] = stacked[c, pl.ds(cz - 1, cx * cy, stride=cz), :]
    total = jnp.zeros((cells, LANES), jnp.float32)
    for a in range(3):
        for b in range(3):
            part = jnp.sum(stacked[3 + a] * stacked[6 + b], axis=1, keepdims=True)
            total = total + jnp.where(code[...] == 3 * a + b, part, 0.0)
    mom[...] = jnp.sum(total, axis=0, keepdims=True)


def exchange_kernel(sizes, fx, fy, fz, mom, hx, hy, hz, gathered, *sems):
    face_send, face_recv, mom_send, mom_recv, own_sem = sems
    index = [lax.axis_index(name) for name in AXES]
    barrier = pltpu.get_barrier_semaphore()
    peers = 0
    for name, me, n in zip(AXES, index, sizes):
        for d in range(1, n):
            pl.semaphore_signal(
                barrier, inc=1, device_id={name: lax.rem(me + d, n)}, device_id_type=MESH
            )
            peers += 1
    pl.semaphore_wait(barrier, peers)

    def moment_copies(level, src, dst):
        name, me, n = AXES[level], index[level], sizes[level]
        base = sum(size - 1 for size in sizes[:level])
        return [
            pltpu.make_async_remote_copy(
                src_ref=src,
                dst_ref=dst,
                send_sem=mom_send.at[base + d - 1],
                recv_sem=mom_recv.at[base + d - 1],
                device_id={name: lax.rem(me + d, n)},
                device_id_type=MESH,
            )
            for d in range(1, n)
        ]

    nx, ny, nz = sizes
    row = (index[0] * ny + index[1]) * nz + index[2]
    own = pltpu.make_async_copy(mom, gathered.at[pl.ds(row, 1)], own_sem)
    own.start()
    first = moment_copies(2, mom, gathered.at[pl.ds(row, 1)])
    for copy in first:
        copy.start()

    def face_copy(axis, face, halo, up):
        me, n = index[axis], sizes[axis]
        slot = 2 * axis + (0 if up else 1)
        return pltpu.make_async_remote_copy(
            src_ref=face.at[1 if up else 0],
            dst_ref=halo.at[0 if up else 1],
            send_sem=face_send.at[slot],
            recv_sem=face_recv.at[slot],
            device_id={AXES[axis]: lax.rem(me + 1, n) if up else lax.rem(me + n - 1, n)},
            device_id_type=MESH,
        )

    pairs = [(0, fx, hx), (1, fy, hy), (2, fz, hz)]

    def start_faces(axis, face, halo):
        @pl.when(index[axis] < sizes[axis] - 1)
        def _():
            face_copy(axis, face, halo, True).start()

        @pl.when(index[axis] > 0)
        def _():
            face_copy(axis, face, halo, False).start()

    for axis, face, halo in pairs:
        start_faces(axis, face, halo)
    own.wait()
    for copy in first:
        copy.wait_recv()
    block = gathered.at[pl.ds((index[0] * ny + index[1]) * nz, nz)]
    second = moment_copies(1, block, block)
    for copy in second:
        copy.start()
    for copy in second:
        copy.wait_recv()
    block = gathered.at[pl.ds(index[0] * ny * nz, ny * nz)]
    third = moment_copies(0, block, block)
    for copy in third:
        copy.start()
    for copy in third:
        copy.wait_recv()
    for axis, face, halo in pairs:

        @pl.when(index[axis] > 0)
        def _():
            face_copy(axis, face, halo, True).wait_recv()

        @pl.when(index[axis] < sizes[axis] - 1)
        def _():
            face_copy(axis, face, halo, False).wait_recv()

        @pl.when(index[axis] < sizes[axis] - 1)
        def _():
            face_copy(axis, face, halo, True).wait_send()

        @pl.when(index[axis] > 0)
        def _():
            face_copy(axis, face, halo, False).wait_send()

    for copy in first + second + third:
        copy.wait_send()


def force_kernel(
    grid, sizes, counts, where, stress, stacked, hx, hy, hz, gathered, centers, groups,
    connect, pos, drag, fields, low, high, ext, staged, rows, turned, sums, near, far, left, right, acc,
):
    cx, cy, cz = grid
    cells = cx * cy * cz
    face = (cy * cz, cx * cz, cx * cy)
    base = [cells]
    for axis in range(3):
        base.append(base[-1] + 2 * face[axis])
    ext[:, 0:cells, :] = stacked[...]
    for axis, halo in enumerate((hx, hy, hz)):
        for side in range(2):
            inside = where[axis] > 0 if side == 0 else where[axis] < sizes[axis] - 1
            start = base[axis] + side * face[axis]
            ext[:, start : start + face[axis], :] = jnp.where(inside, halo[side], 0.0)

    def far_cell(t, carry):
        x, rest = lax.div(t, cy * cz), lax.rem(t, cy * cz)
        y, z = lax.div(rest, cz), lax.rem(rest, cz)
        spot = [
            (where[axis] * grid[axis] + (x, y, z)[axis]).astype(jnp.float32) + 0.5
            for axis in range(3)
        ]
        distance = jnp.full(gathered.shape, SOFTEN_FAR, jnp.float32)
        for axis in range(3):
            gap = spot[axis] - centers[axis]
            distance = distance + gap * gap
        far[pl.ds(t, 1), :] = jnp.sum(
            gathered[...] * lax.rsqrt(distance), axis=0, keepdims=True
        )
        return carry

    lax.fori_loop(0, cells, far_cell, 0)
    lane = lax.broadcasted_iota(jnp.int32, (STEP, LANES), 1)

    def near_cell(t, carry):
        x, rest = lax.div(t, cy * cz), lax.rem(t, cy * cz)
        y, z = lax.div(rest, cz), lax.rem(rest, cz)
        sources = [
            (t, None, 0.0),
            (jnp.where(x < cx - 1, t + cy * cz, base[0] + face[0] + y * cz + z), 0, 1.0),
            (jnp.where(x > 0, t - cy * cz, base[0] + y * cz + z), 0, -1.0),
            (jnp.where(y < cy - 1, t + cz, base[1] + face[1] + x * cz + z), 1, 1.0),
            (jnp.where(y > 0, t - cz, base[1] + x * cz + z), 1, -1.0),
            (jnp.where(z < cz - 1, t + 1, base[2] + face[2] + x * cy + y), 2, 1.0),
            (jnp.where(z > 0, t - 1, base[2] + x * cy + y), 2, -1.0),
        ]
        for k, (row, axis, shift) in enumerate(sources):
            for c in range(9):
                value = ext[c, pl.ds(row, 1), :]
                if k == 0:
                    rows[c : c + 1, :] = value
                if c == axis:
                    value = value + shift
                staged[k * 9 + c] = jnp.broadcast_to(value, (8, LANES))
        turned[...] = rows[...].T
        count = counts[t]

        def chunk(i, carry):
            start = pl.multiple_of(i * STEP, STEP)
            tile = turned[pl.ds(start, STEP), :]
            mine = [
                [jnp.broadcast_to(tile[8 * h : 8 * h + 8, c : c + 1], (8, LANES)) for c in range(9)]
                for h in range(STEP // 8)
            ]
            total = [[jnp.zeros((8, LANES), jnp.float32)] * 3 for _ in range(STEP // 8)]
            for k in range(7):
                other = [staged[k * 9 + c] for c in range(9)]
                for h in range(STEP // 8):
                    me = mine[h]
                    d = [me[c] - other[c] for c in range(3)]
                    radius = d[0] * d[0] + d[1] * d[1] + d[2] * d[2] + SOFTEN_NEAR
                    inverse = lax.rsqrt(radius)
                    bb = me[3] * other[3] + me[4] * other[4] + me[5] * other[5]
                    ll = me[6] * other[6] + me[7] * other[7] + me[8] * other[8]
                    weight = (bb * ll) * (inverse * inverse * inverse)
                    total[h] = [total[h][c] + weight * d[c] for c in range(3)]
            for h in range(STEP // 8):
                out = jnp.zeros((8, LANES), jnp.float32)
                for c in range(3):
                    out = jnp.where(
                        lane[0:8] == c, jnp.sum(total[h][c], axis=1, keepdims=True), out
                    )
                sums[pl.ds(start + 8 * h, 8), :] = out
            return carry

        lax.fori_loop(0, lax.div(count + STEP - 1, STEP), chunk, 0)
        flipped = sums[...].T
        alive = lane[0:1] < count
        for c in range(3):
            near[c, pl.ds(t, 1), :] = jnp.where(alive, flipped[c : c + 1, :], 0.0)
        return carry

    rows[...] = jnp.zeros_like(rows)
    sums[...] = jnp.zeros_like(sums)
    lax.fori_loop(0, cells, near_cell, 0)

    mixed = jnp.dot(
        far[...], groups[...], precision=lax.Precision.HIGHEST, preferred_element_type=jnp.float32
    )
    burgers = [stacked[3 + c] for c in range(3)]
    line = [stacked[6 + c] for c in range(3)]
    pulled = []
    for r in range(3):
        value = 0.0
        for c in range(3):
            sigma = FAR_SCALE * mixed[:, 3 * r + c : 3 * r + c + 1] + stress[r, c]
            value = value + sigma * burgers[c]
        pulled.append(value)
    for c in range(3):
        a, b = (c + 1) % 3, (c + 2) % 3
        total = NEAR_SCALE * near[c] + (pulled[a] * line[b] - pulled[b] * line[a])
        near[c] = 0.5 * total

    node_rows = pos.shape[1]
    half = node_rows // 2
    acc[...] = jnp.zeros_like(acc)
    high_ids = lax.broadcasted_iota(jnp.int32, (half, LANES), 0)
    low_ids = lax.broadcasted_iota(jnp.int32, (2 * LANES, LANES), 0)
    groups_of = cells // 8

    def scatter(step, carry):
        end, block = lax.div(step, groups_of), lax.rem(step, groups_of)
        start = pl.multiple_of(block * 8, 8)
        ids = connect[end, pl.ds(start, 8), :]
        values = [near[c, pl.ds(start, 8), :] for c in range(3)]
        node_row = lax.shift_right_logical(ids, 7)
        upper = node_row >= half
        hi = jnp.where(upper, node_row - half, node_row)
        lo = (ids & (LANES - 1)) + jnp.where(upper, LANES, 0)
        for k in range(8):
            span = slice(k * LANES, (k + 1) * LANES)
            mask = high_ids == hi[k : k + 1, :]
            for c in range(3):
                value = values[c][k : k + 1, :]
                coarse = value.astype(jnp.bfloat16).astype(jnp.float32)
                fine = value - coarse
                left[2 * c * half : (2 * c + 1) * half, span] = jnp.where(mask, coarse, 0.0).astype(
                    jnp.bfloat16
                )
                left[(2 * c + 1) * half : (2 * c + 2) * half, span] = jnp.where(
                    mask, fine, 0.0
                ).astype(jnp.bfloat16)
            right[:, span] = jnp.where(low_ids == lo[k : k + 1, :], 1.0, 0.0).astype(jnp.bfloat16)
        acc[...] += lax.dot_general(
            left[...], right[...], (((1,), (1,)), ((), ())), preferred_element_type=jnp.float32
        )
        return carry

    lax.fori_loop(0, 2 * groups_of, scatter, 0)
    edge = low.shape[1]
    for c in range(3):
        both = acc[2 * c * half : (2 * c + 1) * half, :] + acc[(2 * c + 1) * half : (2 * c + 2) * half, :]
        for s in range(2):
            span = slice(s * half, (s + 1) * half)
            velocity = both[:, s * LANES : (s + 1) * LANES] / drag[span, :]
            fields[3 + c, span, :] = velocity
            fields[c, span, :] = pos[c, span, :] + TIME_STEP * velocity
    for c in range(6):
        low[c] = fields[c, 0:edge, :]
        high[c] = fields[c, node_rows - edge : node_rows, :]


def edge_kernel(n, low, high, below, above, send, recv):
    me = lax.axis_index("gx")
    barrier = pltpu.get_barrier_semaphore()
    after, before = lax.rem(me + 1, n), lax.rem(me + n - 1, n)
    for peer in (after, before):
        pl.semaphore_signal(barrier, inc=1, device_id={"gx": peer}, device_id_type=MESH)
    pl.semaphore_wait(barrier, 2)

    def copy(slot, src, dst, peer):
        return pltpu.make_async_remote_copy(
            src_ref=src,
            dst_ref=dst,
            send_sem=send.at[slot],
            recv_sem=recv.at[slot],
            device_id={"gx": peer},
            device_id_type=MESH,
        )

    @pl.when(me < n - 1)
    def _():
        copy(0, high, below, after).start()

    @pl.when(me > 0)
    def _():
        copy(1, low, above, before).start()

    @pl.when(me < n - 1)
    def _():
        copy(0, high, below, after).wait_send()
        copy(1, low, above, before).wait_recv()

    @pl.when(me > 0)
    def _():
        copy(1, low, above, before).wait_send()
        copy(0, high, below, after).wait_recv()


def assemble_kernel(moves, fields, below, above, out, section):
    node_rows, edge, out_rows = fields.shape[1], below.shape[1], out.shape[1]
    nodes, margin = node_rows * LANES, edge * LANES
    section[:, 0:edge, :] = below[...]
    section[:, edge : edge + node_rows, :] = fields[...]
    section[:, edge + node_rows : 2 * edge + node_rows, :] = above[...]
    up_prev, down_own, up_own, down_next = moves[0], moves[1], moves[2], moves[3]
    kept = nodes - up_own - down_own

    def shifted(c, by, first, count):
        row, turn = lax.div(by, LANES), lax.rem(by, LANES)
        lane = lax.broadcasted_iota(jnp.int32, (count, LANES), 1)
        back = lax.rem(LANES - turn, LANES)
        now = pltpu.roll(section[c, pl.ds(first + row, count), :], back, axis=1)
        later = pltpu.roll(section[c, pl.ds(first + row + 1, count), :], back, axis=1)
        return jnp.where(lane < LANES - turn, now, later)

    tail = out_rows - (4 * edge)
    position = (
        lax.broadcasted_iota(jnp.int32, (out_rows, LANES), 0) * LANES
        + lax.broadcasted_iota(jnp.int32, (out_rows, LANES), 1)
    )
    for c in range(6):
        out[c] = shifted(c, margin + down_own - up_prev, 0, out_rows)
        head = 2 * edge
        value = shifted(c, margin - up_prev, 0, head)
        out[c, 0:head, :] = jnp.where(position[0:head] < up_prev, value, out[c, 0:head, :])
        value = shifted(c, margin + nodes - up_prev - kept, tail, out_rows - tail)
        spot = position[tail:]
        value = jnp.where(spot < up_prev + kept, out[c, tail:out_rows, :], value)
        out[c, tail:out_rows, :] = jnp.where(spot < up_prev + kept + down_next, value, 0.0)


def shards(mesh, offsets, burgers, lines, counts, connect, node_pos, drag, stress, shifts):
    grid = offsets.shape[1:4]
    slots = offsets.shape[4]
    cells = grid[0] * grid[1] * grid[2]
    sizes = tuple(mesh.shape[name] for name in AXES)
    nx, ny, nz = sizes
    devices = nx * ny * nz
    index = [lax.axis_index(name) for name in AXES]
    half = [size // 2 for size in grid]
    local = half[0] * half[1] * half[2]
    nodes = node_pos.shape[4]
    node_rows, edge = nodes // LANES, MIG // LANES
    f32 = jnp.float32

    t = np.arange(cells)
    x, y, z = t // (grid[1] * grid[2]), t // grid[2] % grid[1], t % grid[2]
    coarse = ((x // 2) * half[1] + y // 2) * half[2] + z // 2
    lane = np.arange(LANES)
    code = np.where(lane[None, :] % local == coarse[:, None], lane[None, :] // local, -1)
    device = np.arange(devices)[:, None]
    inner = (lane % local)[None, :]
    centers = np.stack(
        [
            2 * (device // (ny * nz) * half[0] + inner // (half[1] * half[2])) + 1,
            2 * (device // nz % ny * half[1] + inner // half[2] % half[1]) + 1,
            2 * (device % nz * half[2] + inner % half[2]) + 1,
        ]
    ).astype(np.float32)
    groups = (lane[:, None] // local == lane[None, :]).astype(np.float32)

    flat = lambda array: array.reshape(array.shape[0], cells, slots)
    count_rows = counts.reshape(cells)
    face = (grid[1] * grid[2], grid[0] * grid[2], grid[0] * grid[1])
    face_shapes = [jax.ShapeDtypeStruct((2, 9, size, slots), f32) for size in face]

    stacked, fx, fy, fz, moments = pl.pallas_call(
        functools.partial(prep_kernel, grid),
        out_shape=[jax.ShapeDtypeStruct((9, cells, slots), f32)]
        + face_shapes
        + [jax.ShapeDtypeStruct((1, LANES), f32)],
        in_specs=[VM] * 5,
        out_specs=[VM] * 5,
        name="prep",
    )(
        flat(offsets), flat(burgers), flat(lines),
        jnp.broadcast_to(count_rows[:, None], (cells, LANES)), jnp.asarray(code, jnp.int32),
    )

    steps = sum(sizes) - 3
    hx, hy, hz, gathered = pl.pallas_call(
        functools.partial(exchange_kernel, sizes),
        out_shape=face_shapes + [jax.ShapeDtypeStruct((devices, 1, LANES), f32)],
        in_specs=[VM] * 4,
        out_specs=[VM] * 4,
        scratch_shapes=[
            pltpu.SemaphoreType.DMA((6,)),
            pltpu.SemaphoreType.DMA((6,)),
            pltpu.SemaphoreType.DMA((steps,)),
            pltpu.SemaphoreType.DMA((steps,)),
            pltpu.SemaphoreType.DMA,
        ],
        compiler_params=pltpu.CompilerParams(collective_id=0, has_side_effects=True),
        name="exchange",
    )(fx, fy, fz, moments.reshape(1, 1, LANES))

    edge_shape = jax.ShapeDtypeStruct((6, edge, LANES), f32)
    fields, low, high = pl.pallas_call(
        functools.partial(force_kernel, grid, sizes),
        out_shape=[jax.ShapeDtypeStruct((6, node_rows, LANES), f32), edge_shape, edge_shape],
        in_specs=[SM] * 3 + [VM] * 10,
        out_specs=[VM] * 3,
        scratch_shapes=[
            pltpu.VMEM((9, cells + 2 * sum(face), LANES), f32),
            pltpu.VMEM((63, 8, LANES), f32),
            pltpu.VMEM((16, LANES), f32),
            pltpu.VMEM((LANES, 16), f32),
            pltpu.VMEM((LANES, LANES), f32),
            pltpu.VMEM((3, cells, LANES), f32),
            pltpu.VMEM((cells, LANES), f32),
            pltpu.VMEM((3 * node_rows, 8 * LANES), jnp.bfloat16),
            pltpu.VMEM((2 * LANES, 8 * LANES), jnp.bfloat16),
            pltpu.VMEM((3 * node_rows, 2 * LANES), f32),
        ],
        name="forces",
    )(
        count_rows, jnp.stack(index).astype(jnp.int32), stress,
        stacked, hx, hy, hz, gathered.reshape(devices, LANES),
        jnp.asarray(centers), jnp.asarray(groups),
        flat(connect), node_pos.reshape(3, node_rows, LANES), drag.reshape(node_rows, LANES),
    )

    below, above = pl.pallas_call(
        functools.partial(edge_kernel, nx),
        out_shape=[edge_shape, edge_shape],
        in_specs=[VM] * 2,
        out_specs=[VM] * 2,
        scratch_shapes=[pltpu.SemaphoreType.DMA((2,)), pltpu.SemaphoreType.DMA((2,))],
        compiler_params=pltpu.CompilerParams(collective_id=1, has_side_effects=True),
        name="edges",
    )(low, high)

    ix, iy, iz = index
    up_prev = jnp.where(ix > 0, shifts[0][jnp.maximum(ix - 1, 0), iy, iz], 0)
    down_next = jnp.where(ix < nx - 1, shifts[1][jnp.minimum(ix + 1, nx - 1), iy, iz], 0)
    moves = jnp.stack([up_prev, shifts[1][ix, iy, iz], shifts[0][ix, iy, iz], down_next])
    out_rows = node_rows + 2 * edge
    result = pl.pallas_call(
        assemble_kernel,
        out_shape=jax.ShapeDtypeStruct((6, out_rows, LANES), f32),
        in_specs=[SM] + [VM] * 3,
        out_specs=VM,
        scratch_shapes=[pltpu.VMEM((6, out_rows + 4 * edge, LANES), f32)],
        name="assemble",
    )(moves.astype(jnp.int32), fields, below, above)
    return result.reshape(6, 1, 1, 1, out_rows * LANES)


def solution(mesh):
    return jax.shard_map(
        functools.partial(shards, mesh),
        mesh=mesh,
        in_specs=(
            P(None, "gx", "gy", "gz", None),
            P(None, "gx", "gy", "gz", None),
            P(None, "gx", "gy", "gz", None),
            P("gx", "gy", "gz"),
            P(None, "gx", "gy", "gz", None),
            P(None, "gx", "gy", "gz", None),
            P("gx", "gy", "gz", None),
            P(),
            P(),
        ),
        out_specs=P(None, "gx", "gy", "gz", None),
        check_vma=False,
    )
```

time: 344 us -> 121 us (0.35)
  other arithmetic: 206 us -> 2.58 us
  Pallas kernels: 0 us -> 116 us
  local copies, waits for them, and re-layouts: 62.4 us -> 2.82 us
  blocking collectives: 41.1 us -> 0 us
  starting transfers between devices: 22.4 us -> 0 us
  waiting for transfers between devices: 4.33 us -> 0 us
    pallas_call x0 -> x5, Pallas kernels: none -> 116 us  [the longest x1 91.3 us: shards(): pl.pallas_call(functools.partial(force_kernel, grid, sizes), out_shape=[j...]
    reduce_sum x7 -> x0, other arithmetic: 94.3 us -> none  [the longest x6 94.2 us: pair_term(): jnp.sum(weight * deltas[axis_id], axis=-1)]
    scatter-add x1 -> x0, other arithmetic: 89.8 us -> none  [shards(): jax.ops.segment_sum(values, connect.reshape(-1), num_segments=nodes)]
    all_gather x1 -> x0, blocking collectives: 41.1 us -> none  [shards(): lax.all_gather(own_moments.reshape(9, 1, local_count), ('gx', 'gy', 'gz')...]
    gather x1 -> x0, local copies, waits for them, and re-layouts: 33.3 us -> none  [shards(): result = jnp.where(live[None], jnp.take(sectioning, source, axis=1), 0.0)]
    ppermute x8 -> x0, starting transfers between devices: 22.4 us -> none  [the longest x3 12.7 us: with_halo(): lax.ppermute(tail, axis, [(i, (i + 1) % count) for i in range(ends)])]
    select_n x4 -> x0, other arithmetic: 11.6 us -> none  [the longest x2 11.5 us: shards(): result = jnp.where(live[None], jnp.take(sectioning, source, axis=1), 0.0)]
    add x3 -> x0, other arithmetic: 6.09 us -> none  [the longest x1 6.07 us: shards(): node_pos.reshape(3, nodes) + TIME_STEP * velocity]
  transfers between devices with their start and end apart: 8 -> 0, of which waited for: 2 -> 0; matrix products, arithmetic and copies ran while one was open for 21% -> 0% of each run, Pallas kernels for 0% -> 0%
where the time goes in v1:
time: 121 us; the launch traced here: 122 us
  Pallas kernels  116 us (96%)
  local copies, waits for them, and re-layouts  2.82 us (2%)
  other arithmetic  2.58 us (2%)
  between operations  1.31 us (1%)
    pallas_call x1, Pallas kernels, shards(): pl.pallas_call(functools.partial(force_kernel, grid, sizes), out_shape=[j...  91.3 us
    pallas_call x1, Pallas kernels, shards(): pl.pallas_call(functools.partial(exchange_kernel, sizes), out_shape=face_...  15.5 us
    pallas_call x1, Pallas kernels, shards(): pl.pallas_call(functools.partial(edge_kernel, nx), out_shape=[edge_shape,...  5.08 us

profile of v1, /device:TPU:0, one launch (start us, length us, event | category | flops | bytes accessed | tf_op | source)
XLA Modules:
  0.0 122.4 jit_solution(3146354202199463615)
XLA Ops:
  0.0 0.8 reshape.39.counts
  0.8 0.0 copy-start.1
  0.8 0.7 broadcast_in_dim.2.counts
  1.5 0.0 copy-done.1
  1.5 1.9 %prep.1 = (f32[9,64,128]{2,1,0:T(8,128)}, f32[2,9,16,128]{3,2,1,0:T(8,128)}, f32[2,9,16,128]{3,2,1,0:T(8,128)}, f32[2,9,16,128]{3,2,1,0:T(8,128)}, f32[1,128]{1,0:T(1,128)}) custom-call(f32[3,64,128]{2,1,0:T(8,128)} %bitcast.19, f32[3,64,128]{2,1,0:T(8,128)} %bitcast.20, f32[3,64,128]{2,1,0:T(8,128)} %bitcast.21, s32[64,128]{1,0:T(8,128)} %broadcast_in_dim.2.counts, ...), custom_call_target="tpu_custom_call" | custom-call | tf_op jit(solution)/shard_map/prep/pallas_call | solution.py:418
  3.4 15.5 %exchange.1 = (f32[2,9,16,128]{3,2,1,0:T(8,128)}, f32[2,9,16,128]{3,2,1,0:T(8,128)}, f32[2,9,16,128]{3,2,1,0:T(8,128)}, f32[32,1,128]{2,1,0:T(1,128)}) custom-call(f32[2,9,16,128]{3,2,1,0:T(8,128)} %get-tuple-element.20.fx, f32[2,9,16,128]{3,2,1,0:T(8,128)} %get-tuple-element.21.fy, f32[2,9,16,128]{3,2,1,0:T(8,128)} %get-tuple-element.22.fz, ...), custom_call_target="tpu_custom_call" | custom-call | tf_op jit(solution)/shard_map/exchange/pallas_call | solution.py:432
  18.9 0.7 pad_add_fusion.1.where
  19.6 91.3 %forces.1 = (f32[6,64,128]{2,1,0:T(8,128)}, f32[6,4,128]{2,1,0:T(4,128)}, f32[6,4,128]{2,1,0:T(4,128)}) custom-call(s32[64]{0:T(128)} %copy-done.1, s32[3]{0:T(128)} %pad_add_fusion.1.where, f32[3,3]{1,0:T(4,128)} %stress.1, f32[9,64,128]{2,1,0:T(8,128)} %get-tuple-element.19.stacked, f32[2,9,16,128]{3,2,1,0:T(8,128)} %get-tuple-element.24.hx, ...), custom_call_target="tpu_custom_call" | custom-call | tf_op jit(solution)/shard_map/forces/pallas_call | solution.py:449
  110.9 5.1 %edges.1 = (f32[6,4,128]{2,1,0:T(4,128)}, f32[6,4,128]{2,1,0:T(4,128)}) custom-call(f32[6,4,128]{2,1,0:T(4,128)} %get-tuple-element.29.low, f32[6,4,128]{2,1,0:T(4,128)} %get-tuple-element.30.high), custom_call_target="tpu_custom_call" | custom-call | tf_op jit(solution)/shard_map/edges/pallas_call | solution.py:474
  116.0 0.0 copy-start
  116.0 0.7 copy-done
  116.7 0.6 constant_dynamic-slice_fusion.2
  118.6 1.9 %pad_add_fusion.moves = s32[4]{0:T(128)} fusion(s32[1]{0:T(128)} %bitcast.5, s32[1]{0:T(128)} %bitcast.3, s32[1]{0:T(128)} %bitcast.2, s32[1]{0:T(128)} %bitcast.1), kind=kLoop, calls=%fused_computation.4 | loop fusion | flops 12 | bytes 32 | tf_op jit(solution)/shard_map/stack | solution.py:487
  120.6 1.9 %assemble.1 = f32[6,72,128]{2,1,0:T(8,128)} custom-call(s32[4]{0:T(128)} %pad_add_fusion.moves, f32[6,64,128]{2,1,0:T(8,128)} %get-tuple-element.28.fields, f32[6,4,128]{2,1,0:T(4,128)} %get-tuple-element.31.below, f32[6,4,128]{2,1,0:T(4,128)} %get-tuple-element.32.above), custom_call_target="tpu_custom_call" | custom-call | tf_op jit(solution)/shard_map/assemble/pallas_call | solution.py:489
  (1 shorter events, 0.0 us)
Async XLA Ops:
  0.8 0.7 copy-start.1
  116.0 0.7 copy-start

commit v2 on v1

--- a/solution.py
+++ b/solution.py
@@ -20,6 +20,7 @@
 SM = pl.BlockSpec(memory_space=pltpu.SMEM)
 LANES = 128
 STEP = 16
+ROWS = 16
 
 
 def prep_kernel(grid, off, bur, lin, counts, code, stacked, faces_x, faces_y, faces_z, mom):
@@ -147,21 +148,30 @@
 
 
 def force_kernel(
-    grid, sizes, counts, where, stress, stacked, hx, hy, hz, gathered, centers, groups,
-    connect, pos, drag, fields, low, high, ext, staged, rows, turned, sums, near, far, left, right, acc,
+    grid, sizes, counts, stress, stacked, hx, hy, hz, gathered, centers, groups,
+    connect, pos, drag, fields, low, high, ext, packed, staged, turned, sums, near, far, left, right, acc,
 ):
     cx, cy, cz = grid
     cells = cx * cy * cz
+    where = [lax.axis_index(name) for name in AXES]
     face = (cy * cz, cx * cz, cx * cy)
     base = [cells]
     for axis in range(3):
         base.append(base[-1] + 2 * face[axis])
-    ext[:, 0:cells, :] = stacked[...]
-    for axis, halo in enumerate((hx, hy, hz)):
-        for side in range(2):
-            inside = where[axis] > 0 if side == 0 else where[axis] < sizes[axis] - 1
-            start = base[axis] + side * face[axis]
-            ext[:, start : start + face[axis], :] = jnp.where(inside, halo[side], 0.0)
+    for c in range(9):
+        ext[pl.ds(c, cells, stride=ROWS), :] = stacked[c]
+        for axis, halo in enumerate((hx, hy, hz)):
+            for side in range(2):
+                start = base[axis] + side * face[axis]
+                ext[pl.ds(start * ROWS + c, face[axis], stride=ROWS), :] = halo[side, c]
+    full = ext.shape[1]
+    outer = [
+        (
+            jnp.where(where[axis] > 0, full, 0),
+            jnp.where(where[axis] < sizes[axis] - 1, full, 0),
+        )
+        for axis in range(3)
+    ]
 
     def far_cell(t, carry):
         x, rest = lax.div(t, cy * cz), lax.rem(t, cy * cz)
@@ -180,40 +190,57 @@
         return carry
 
     lax.fori_loop(0, cells, far_cell, 0)
-    lane = lax.broadcasted_iota(jnp.int32, (STEP, LANES), 1)
+    lane = lax.broadcasted_iota(jnp.int32, (ROWS, LANES), 1)
+    sub = lax.broadcasted_iota(jnp.int32, (ROWS, LANES), 0)
 
     def near_cell(t, carry):
         x, rest = lax.div(t, cy * cz), lax.rem(t, cy * cz)
         y, z = lax.div(rest, cz), lax.rem(rest, cz)
-        sources = [
-            (t, None, 0.0),
-            (jnp.where(x < cx - 1, t + cy * cz, base[0] + face[0] + y * cz + z), 0, 1.0),
-            (jnp.where(x > 0, t - cy * cz, base[0] + y * cz + z), 0, -1.0),
-            (jnp.where(y < cy - 1, t + cz, base[1] + face[1] + x * cz + z), 1, 1.0),
-            (jnp.where(y > 0, t - cz, base[1] + x * cz + z), 1, -1.0),
-            (jnp.where(z < cz - 1, t + 1, base[2] + face[2] + x * cy + y), 2, 1.0),
-            (jnp.where(z > 0, t - 1, base[2] + x * cy + y), 2, -1.0),
-        ]
-        for k, (row, axis, shift) in enumerate(sources):
+        spot = (x, y, z)
+        count = counts[t]
+        mine_tile = ext[pl.ds(pl.multiple_of(t * ROWS, ROWS), ROWS), :]
+        turned[...] = mine_tile.T
+        sources = [(t, count, None, 0.0)]
+        pitch = (cy * cz, cz, 1)
+        offset = (y * cz + z, x * cz + z, x * cy + y)
+        for axis in range(3):
+            for side, step in ((1, 1.0), (0, -1.0)):
+                inner = spot[axis] < grid[axis] - 1 if side else spot[axis] > 0
+                beside = t + pitch[axis] if side else t - pitch[axis]
+                beside = jnp.where(inner, beside, 0)
+                row = jnp.where(inner, beside, base[axis] + side * face[axis] + offset[axis])
+                number = jnp.where(inner, counts[beside], outer[axis][side])
+                sources.append((row, number, axis, step))
+        for q in range(packed.shape[0]):
+            packed[q] = jnp.zeros((ROWS, LANES), jnp.float32)
+        fill = jnp.int32(0)
+        for row, number, axis, step in sources:
+            tile = ext[pl.ds(pl.multiple_of(row * ROWS, ROWS), ROWS), :]
+            if axis is not None:
+                tile = jnp.where(sub == axis, tile + step, tile)
+            turn, q = lax.rem(fill, LANES), lax.div(fill, LANES)
+            rolled = pltpu.roll(tile, turn, axis=1)
+            packed[q] += jnp.where((lane >= turn) & (lane < turn + number), rolled, 0.0)
+            packed[q + 1] += jnp.where(lane < turn + number - LANES, rolled, 0.0)
+            fill = fill + number
+        used = lax.div(fill + LANES - 1, LANES)
+
+        def spread(q, carry):
             for c in range(9):
-                value = ext[c, pl.ds(row, 1), :]
-                if k == 0:
-                    rows[c : c + 1, :] = value
-                if c == axis:
-                    value = value + shift
-                staged[k * 9 + c] = jnp.broadcast_to(value, (8, LANES))
-        turned[...] = rows[...].T
-        count = counts[t]
-
-        def chunk(i, carry):
+                staged[q * 9 + c] = jnp.broadcast_to(packed[q, c : c + 1, :], (8, LANES))
+            return carry
+
+        lax.fori_loop(0, used, spread, 0)
+
+        def chunk(n, i, carry):
             start = pl.multiple_of(i * STEP, STEP)
             tile = turned[pl.ds(start, STEP), :]
             mine = [
                 [jnp.broadcast_to(tile[8 * h : 8 * h + 8, c : c + 1], (8, LANES)) for c in range(9)]
                 for h in range(STEP // 8)
             ]
-            total = [[jnp.zeros((8, LANES), jnp.float32)] * 3 for _ in range(STEP // 8)]
-            for k in range(7):
+            total = [[None] * 3 for _ in range(STEP // 8)]
+            for k in range(n):
                 other = [staged[k * 9 + c] for c in range(9)]
                 for h in range(STEP // 8):
                     me = mine[h]
@@ -223,24 +250,31 @@
                     bb = me[3] * other[3] + me[4] * other[4] + me[5] * other[5]
                     ll = me[6] * other[6] + me[7] * other[7] + me[8] * other[8]
                     weight = (bb * ll) * (inverse * inverse * inverse)
-                    total[h] = [total[h][c] + weight * d[c] for c in range(3)]
+                    for c in range(3):
+                        term = weight * d[c]
+                        total[h][c] = term if k == 0 else total[h][c] + term
             for h in range(STEP // 8):
                 out = jnp.zeros((8, LANES), jnp.float32)
                 for c in range(3):
                     out = jnp.where(
                         lane[0:8] == c, jnp.sum(total[h][c], axis=1, keepdims=True), out
                     )
-                sums[pl.ds(start + 8 * h, 8), :] = out
+                sums[pl.ds(start + 8 * h, 8), :] = out[:, 0:8]
             return carry
 
-        lax.fori_loop(0, lax.div(count + STEP - 1, STEP), chunk, 0)
+        chunks = lax.div(count + STEP - 1, STEP)
+        for n in range(1, 8):
+
+            @pl.when(used == n)
+            def _():
+                lax.fori_loop(0, chunks, functools.partial(chunk, n), 0)
+
         flipped = sums[...].T
         alive = lane[0:1] < count
         for c in range(3):
             near[c, pl.ds(t, 1), :] = jnp.where(alive, flipped[c : c + 1, :], 0.0)
         return carry
 
-    rows[...] = jnp.zeros_like(rows)
     sums[...] = jnp.zeros_like(sums)
     lax.fori_loop(0, cells, near_cell, 0)
 
@@ -347,13 +381,18 @@
         copy(0, high, below, after).wait_recv()
 
 
-def assemble_kernel(moves, fields, below, above, out, section):
+def assemble_kernel(sizes, moves, fields, below, above, out, section):
     node_rows, edge, out_rows = fields.shape[1], below.shape[1], out.shape[1]
     nodes, margin = node_rows * LANES, edge * LANES
     section[:, 0:edge, :] = below[...]
     section[:, edge : edge + node_rows, :] = fields[...]
     section[:, edge + node_rows : 2 * edge + node_rows, :] = above[...]
-    up_prev, down_own, up_own, down_next = moves[0], moves[1], moves[2], moves[3]
+    nx, ny, nz = sizes
+    ix, iy, iz = [lax.axis_index(name) for name in AXES]
+    at = lambda k, slab: moves[((k * nx + slab) * ny + iy) * nz + iz]
+    up_own, down_own = at(0, ix), at(1, ix)
+    up_prev = jnp.where(ix > 0, at(0, jnp.maximum(ix - 1, 0)), 0)
+    down_next = jnp.where(ix < nx - 1, at(1, jnp.minimum(ix + 1, nx - 1)), 0)
     kept = nodes - up_own - down_own
 
     def shifted(c, by, first, count):
@@ -387,7 +426,6 @@
     sizes = tuple(mesh.shape[name] for name in AXES)
     nx, ny, nz = sizes
     devices = nx * ny * nz
-    index = [lax.axis_index(name) for name in AXES]
     half = [size // 2 for size in grid]
     local = half[0] * half[1] * half[2]
     nodes = node_pos.shape[4]
@@ -449,14 +487,14 @@
     fields, low, high = pl.pallas_call(
         functools.partial(force_kernel, grid, sizes),
         out_shape=[jax.ShapeDtypeStruct((6, node_rows, LANES), f32), edge_shape, edge_shape],
-        in_specs=[SM] * 3 + [VM] * 10,
+        in_specs=[SM] * 2 + [VM] * 10,
         out_specs=[VM] * 3,
         scratch_shapes=[
-            pltpu.VMEM((9, cells + 2 * sum(face), LANES), f32),
+            pltpu.VMEM(((cells + 2 * sum(face)) * ROWS, LANES), f32),
+            pltpu.VMEM((8, ROWS, LANES), f32),
             pltpu.VMEM((63, 8, LANES), f32),
-            pltpu.VMEM((16, LANES), f32),
-            pltpu.VMEM((LANES, 16), f32),
-            pltpu.VMEM((LANES, LANES), f32),
+            pltpu.VMEM((LANES, ROWS), f32),
+            pltpu.VMEM((LANES, 8), f32),
             pltpu.VMEM((3, cells, LANES), f32),
             pltpu.VMEM((cells, LANES), f32),
             pltpu.VMEM((3 * node_rows, 8 * LANES), jnp.bfloat16),
@@ -465,7 +503,7 @@
         ],
         name="forces",
     )(
-        count_rows, jnp.stack(index).astype(jnp.int32), stress,
+        count_rows, stress,
         stacked, hx, hy, hz, gathered.reshape(devices, LANES),
         jnp.asarray(centers), jnp.asarray(groups),
         flat(connect), node_pos.reshape(3, node_rows, LANES), drag.reshape(node_rows, LANES),
@@ -481,19 +519,15 @@
         name="edges",
     )(low, high)
 
-    ix, iy, iz = index
-    up_prev = jnp.where(ix > 0, shifts[0][jnp.maximum(ix - 1, 0), iy, iz], 0)
-    down_next = jnp.where(ix < nx - 1, shifts[1][jnp.minimum(ix + 1, nx - 1), iy, iz], 0)
-    moves = jnp.stack([up_prev, shifts[1][ix, iy, iz], shifts[0][ix, iy, iz], down_next])
     out_rows = node_rows + 2 * edge
     result = pl.pallas_call(
-        assemble_kernel,
+        functools.partial(assemble_kernel, sizes),
         out_shape=jax.ShapeDtypeStruct((6, out_rows, LANES), f32),
         in_specs=[SM] + [VM] * 3,
         out_specs=VM,
         scratch_shapes=[pltpu.VMEM((6, out_rows + 4 * edge, LANES), f32)],
         name="assemble",
-    )(moves.astype(jnp.int32), fields, below, above)
+    )(shifts.reshape(-1), fields, below, above)
     return result.reshape(6, 1, 1, 1, out_rows * LANES)
 
 

time: 121 us -> 114 us (0.942)
  the two profiles are of different devices: /device:TPU:0 before, /device:TPU:22 now
where the time goes in v2:
time: 114 us; the launch traced here: 112 us
  Pallas kernels  110 us (96%)
  local copies, waits for them, and re-layouts  2.08 us (2%)
    pallas_call x1, Pallas kernels, shards(): pl.pallas_call(functools.partial(force_kernel, grid, sizes), out_shape=[j...  89.4 us
    pallas_call x1, Pallas kernels, shards(): pl.pallas_call(functools.partial(exchange_kernel, sizes), out_shape=face_...  11.8 us
    pallas_call x1, Pallas kernels, shards(): pl.pallas_call(functools.partial(edge_kernel, nx), out_shape=[edge_shape,...  5.1 us

profile of v2, /device:TPU:22, one launch (start us, length us, event | category | flops | bytes accessed | tf_op | source)
XLA Modules:
  0.0 112.2 jit_solution(16241538684789000085)
XLA Ops:
  0.0 0.8 reshape.35.counts
  0.8 0.0 copy-start.1
  0.8 0.7 broadcast_in_dim.2.counts
  1.5 0.0 copy-done.1
  1.5 1.9 %prep.1 = (f32[9,64,128]{2,1,0:T(8,128)}, f32[2,9,16,128]{3,2,1,0:T(8,128)}, f32[2,9,16,128]{3,2,1,0:T(8,128)}, f32[2,9,16,128]{3,2,1,0:T(8,128)}, f32[1,128]{1,0:T(1,128)}) custom-call(f32[3,64,128]{2,1,0:T(8,128)} %bitcast.9, f32[3,64,128]{2,1,0:T(8,128)} %bitcast.10, f32[3,64,128]{2,1,0:T(8,128)} %bitcast.11, s32[64,128]{1,0:T(8,128)} %broadcast_in_dim.2.counts, ...), custom_call_target="tpu_custom_call" | custom-call | tf_op jit(solution)/shard_map/prep/pallas_call | solution.py:456
  3.4 11.8 %exchange.1 = (f32[2,9,16,128]{3,2,1,0:T(8,128)}, f32[2,9,16,128]{3,2,1,0:T(8,128)}, f32[2,9,16,128]{3,2,1,0:T(8,128)}, f32[32,1,128]{2,1,0:T(1,128)}) custom-call(f32[2,9,16,128]{3,2,1,0:T(8,128)} %get-tuple-element.20.fx, f32[2,9,16,128]{3,2,1,0:T(8,128)} %get-tuple-element.21.fy, f32[2,9,16,128]{3,2,1,0:T(8,128)} %get-tuple-element.22.fz, ...), custom_call_target="tpu_custom_call" | custom-call | tf_op jit(solution)/shard_map/exchange/pallas_call | solution.py:470
  15.3 89.4 %forces.1 = (f32[6,64,128]{2,1,0:T(8,128)}, f32[6,4,128]{2,1,0:T(4,128)}, f32[6,4,128]{2,1,0:T(4,128)}) custom-call(s32[64]{0:T(128)} %copy-done.1, f32[3,3]{1,0:T(4,128)} %stress.1, f32[9,64,128]{2,1,0:T(8,128)} %get-tuple-element.19.stacked, f32[2,9,16,128]{3,2,1,0:T(8,128)} %get-tuple-element.24.hx, f32[2,9,16,128]{3,2,1,0:T(8,128)} %get-tuple-element.25.hy, ...), custom_call_target="tpu_custom_call" | custom-call | tf_op jit(solution)/shard_map/forces/pallas_call | solution.py:487
  104.6 0.0 copy-start
  104.6 5.1 %edges.1 = (f32[6,4,128]{2,1,0:T(4,128)}, f32[6,4,128]{2,1,0:T(4,128)}) custom-call(f32[6,4,128]{2,1,0:T(4,128)} %get-tuple-element.29.low, f32[6,4,128]{2,1,0:T(4,128)} %get-tuple-element.30.high), custom_call_target="tpu_custom_call" | custom-call | tf_op jit(solution)/shard_map/edges/pallas_call | solution.py:512
  109.7 0.0 copy-done
  109.7 0.6 reshape.34.moves
  110.3 1.9 %assemble.1 = f32[6,72,128]{2,1,0:T(8,128)} custom-call(s32[64]{0:T(128)} %reshape.34.moves, f32[6,64,128]{2,1,0:T(8,128)} %get-tuple-element.28.fields, f32[6,4,128]{2,1,0:T(4,128)} %get-tuple-element.31.below, f32[6,4,128]{2,1,0:T(4,128)} %get-tuple-element.32.above), custom_call_target="tpu_custom_call" | custom-call | tf_op jit(solution)/shard_map/assemble/pallas_call | solution.py:523
Async XLA Ops:
  0.8 0.7 copy-start.1
  104.6 5.1 %copy-start = (s32[2,2,4,4]{3,2,1,0:T(4,128)S(1)}, s32[2,2,4,4]{3,2,1,0:T(4,128)}, u32[]{:S(2)}) copy-start(s32[2,2,4,4]{3,2,1,0:T(4,128)} %param.20) | copy-start | bytes 772
